TPU v7x, 128 devices: a whole 4x4x4 slice. The times are simulated.
128 devices in a mesh: bank: 4 (over y_hi, core), gal: 32 (over z, y_lo, x).
Axes of the slice: x: 4, y: 4 (y_hi: 2, y_lo: 2; y = y_hi * 2 + y_lo), z: 4, core: 2. Of those that a mesh axis runs over, the one named last changes fastest.
Arguments:
- querybank: bfloat16 [16384, 512], P(('bank', 'gal')), may hold values from -80 to 80
- gallery: bfloat16 [131072, 512], P('gal'), may hold values from -80 to 80
- test_queries: bfloat16 [2048, 512], P(('bank', 'gal')), may hold values from -80 to 80
Outputs:
- retrieval: float32 [2048, 32, 4096], P(None, 'gal', 'bank')
All inputs are finite; a program needn't handle non-finite values.
Results may differ from a plain program's by a relative error of at most 0.0017.
Values may be sent and summed in bfloat16 or wider, within the bound.
A program may use at most 64 MiB of HBM per device.

v0:
```python
import jax
import jax.numpy as jnp
from jax import lax
from jax.sharding import PartitionSpec as P

inverse_temp = 20.0
epsilon = 1e-06


def unit_rows(values):
    wide = values.astype(jnp.float32)
    return (wide * lax.rsqrt(jnp.sum(wide * wide, axis=-1, keepdims=True) + epsilon)).astype(
        jnp.bfloat16
    )


def exp_sums(piece, clips_t):
    rows = piece.shape[0]
    blocks = piece.reshape(rows // 512, 512, piece.shape[1])

    def one_block(total, block):
        sims = jnp.dot(block, clips_t, preferred_element_type=jnp.float32)
        return (total + jnp.sum(jnp.exp(inverse_temp * sims), axis=0), None)

    start_total = jnp.zeros((clips_t.shape[1],), jnp.float32)
    total, unused = lax.scan(one_block, start_total, blocks)
    return total


def local(querybank, gallery, test_queries):
    clips_t = unit_rows(gallery).T
    captions = unit_rows(querybank)
    tests = unit_rows(test_queries)
    groups = lax.axis_size("bank")
    count = captions.shape[0] * lax.axis_size("gal") * groups
    share = clips_t.shape[1] // groups
    partial_sums = exp_sums(lax.all_gather(captions, "gal", axis=0, tiled=True), clips_t)
    totals = lax.psum(partial_sums, "bank")
    mine = lax.dynamic_slice_in_dim(totals, lax.axis_index("bank") * share, share, 0)
    every_test = lax.all_gather(tests, ("bank", "gal"), axis=0, tiled=True)
    columns = lax.dynamic_slice_in_dim(clips_t, lax.axis_index("bank") * share, share, 1)
    sims = jnp.dot(every_test, columns, preferred_element_type=jnp.float32)
    result = inverse_temp * sims - jnp.log(mine / count)[None, :]
    return result[:, None, :]


def solution(mesh):
    placed = (P(("bank", "gal"), None), P("gal", None), P(("bank", "gal"), None))
    return jax.shard_map(
        local, mesh=mesh, in_specs=placed, out_specs=P(None, "gal", "bank"), check_vma=False
    )
```

profile of v0, /device:TPU:1, one launch (start us, length us, event | category | flops | bytes accessed | tf_op | source)
XLA Modules:
  0.0 500.7 jit_solution(5182620168477035748)
XLA Ops:
  6.5 0.0 all-gather.5.cloned.1.call-start
  6.5 1.0 fusion.6
  7.6 1.6 fusion.7
  9.2 0.0 all-gather.5.cloned.1.call-update
  9.2 0.0 all-gather.3.cloned.1.call-start
  9.3 0.8 fusion.8
  10.1 1.4 fusion.9
  11.5 0.0 all-gather.3.cloned.1.call-update
  11.6 6.3 %copy.4 = bf16[4096,512]{0,1:T(8,128)(2,1)} copy(bf16[4096,512]{1,0:T(8,128)(2,1)} %param.6) | data formatting | bytes 8388608 | tf_op args[1]
  17.9 0.0 copy-start
  17.9 3.2 fusion.3
  21.1 0.2 copy-done
  21.3 2.9 fusion.13
  24.2 2.8 fusion.4
  27.0 122.1 %all-gather.5.cloned.1.call-done = bf16[4096,512]{1,0:T(8,128)(2,1)} async-done(((bf16[128,512]{1,0:T(8,128)(2,1)}), bf16[4096,512]{1,0:T(8,128)(2,1)}) %all-gather.5.cloned.1.call-update) | async-done | bytes 4194320 | tf_op jit(solution)/shard_map/all_gather | solution.py:37
  149.1 38.5 %while.11 = (s32[]{:T(128)}, f32[4096]{0:T(1024)S(1)}, bf16[8,512,512]{2,1,0:T(8,128)(2,1)}, bf16[512,4096]{1,0:T(8,128)(2,1)}, s32[]{:T(128)}, /*index=5*/s32[]{:T(128)}) while((s32[]{:T(128)}, f32[4096]{0:T(1024)S(1)}, bf16[8,512,512]{2,1,0:T(8,128)(2,1)}, bf16[512,4096]{1,0:T(8,128)(2,1)}, s32[]{:T(128)}, ...), condition=%wide.region_5.6_spmd.clone, body=%wide.region_3.5_spmd.clone.sunk | while | flops 2151682048 | bytes 4784219 | solution.py:26
  149.1 4.8 exponential_reduce_fusion.2
  153.9 4.8 exponential_reduce_fusion.2
  158.7 4.8 exponential_reduce_fusion.2
  163.5 4.8 exponential_reduce_fusion.2
  168.4 4.8 exponential_reduce_fusion.2
  173.2 4.8 exponential_reduce_fusion.2
  178.0 4.8 exponential_reduce_fusion.2
  182.8 4.8 exponential_reduce_fusion.2
  187.6 32.3 %psum.7 = f32[4096]{0:T(1024)S(1)} all-reduce(f32[4096]{0:T(1024)S(1)} %get-tuple-element.27), channel_id=1, replica_groups=mesh['bank'=4,'gal'=32] {'bank'}, use_global_device_ids=true, to_apply=%region_6.7 | all-reduce | flops 4096 | bytes 32768 | tf_op jit(solution)/shard_map/psum | solution.py:38
  219.9 253.6 %all-gather.3.cloned.1.call-done = bf16[2048,512]{1,0:T(8,128)(2,1)} async-done(((bf16[16,512]{1,0:T(8,128)(2,1)}), bf16[2048,512]{1,0:T(8,128)(2,1)}) %all-gather.3.cloned.1.call-update) | async-done | bytes 2097168 | tf_op jit(solution)/shard_map/all_gather | solution.py:40
  473.5 4.2 subtract_bitcast_fusion
  477.8 16.1 %copy.5 = f32[2048,1,1024]{2,1,0:T(1,128)} copy(f32[2048,1,1024]{2,0,1:T(8,128)S(1)} %subtract_bitcast_fusion) | data formatting | bytes 16777216 | tf_op jit(solution)/shard_map/broadcast_in_dim | solution.py:44
  (13 shorter events, 0.1 us)
Async XLA Ops:
  6.5 142.6 %all-gather.5.cloned.1.call-start = ((), (), s32[]{:S(2)}) async-start(), calls=%async_computation.1 | async-start | bytes 4325376 | tf_op jit(solution)/shard_map/all_gather | solution.py:37
  9.2 464.3 %all-gather.3.cloned.1.call-start = ((), (), s32[]{:S(2)}) async-start(), calls=%async_computation | async-start | bytes 2113536 | tf_op jit(solution)/shard_map/all_gather | solution.py:40
  17.9 3.4 copy-start
Sparse Core Ops, SparseCore 0:
  9.4 139.7 all-gather.4
  150.8 322.6 all-gather.2
where the time goes:
time: 501 us
  waiting for transfers between devices  376 us (75%)
  matrix products  42.4 us (8%)
  blocking collectives  32.3 us (6%)
  local copies, waits for them, and re-layouts  22.7 us (5%)
  other arithmetic  13.9 us (3%)
  between operations  13.5 us (3%)
    all_gather x1, waiting for transfers between devices, local(): every_test = lax.all_gather(tests, ('bank', 'gal'), axis=0, tiled=True)  254 us
    all_gather x1, waiting for transfers between devices, local(): lax.all_gather(captions, 'gal', axis=0, tiled=True)  122 us
    dot_general x8, matrix products, one_block(): sims = jnp.dot(block, clips_t, preferred_element_type=jnp.float32)  38.2 us
    psum x1, blocking collectives, local(): totals = lax.psum(partial_sums, 'bank')  32.3 us
    broadcast_in_dim x1, local copies, waits for them, and re-layouts, local(): return result[:, None, :]  16.1 us
  transfers between devices with their start and end apart: 2, of which 2 were waited for; matrix products, arithmetic and copies ran while one was open for 11% of the time, Pallas kernels for 0%

commit v1 on v0

v1 whole, which is shorter than its diff:
```python
import functools
import math

import jax
import jax.numpy as jnp
from jax import lax
from jax.experimental import pallas as pl
from jax.experimental.pallas import tpu as pltpu
from jax.sharding import PartitionSpec as P

MESH = pl.DeviceIdType.MESH
inverse_temp = 20.0
epsilon = 1e-06
exp2_scale = inverse_temp * math.log2(math.e)

D = 512
PIECE = 64
GROUP = 4
RING = 4


def piece_table():
    ring_hops = (0, 1, 2, 1)
    pieces = [
        (kind, dy, p1, p2)
        for dy in range(2)
        for p1 in range(RING)
        for p2 in range(RING)
        for kind in range(2)
    ]

    def depth(piece):
        return piece[1] + ring_hops[piece[2]] + ring_hops[piece[3]]

    def way(piece):
        kind, dy, p1, p2 = piece
        if p2:
            side = p2 if p2 != 2 else (1 if (dy + p1) % 2 == 0 else 3)
            parent = (kind, dy, p1, (p2 - side) % RING)
            return parent, ("x", "z")[1 - kind], side
        if p1:
            side = p1 if p1 != 2 else (1 if dy == 0 else 3)
            parent = (kind, dy, (p1 - side) % RING, 0)
            return parent, ("x", "z")[kind], side
        if dy:
            return (kind, 0, 0, 0), "y", 1
        return None

    pieces.sort(key=lambda q: (depth(q), q[3] != 0, q[2] != 0, q[1], q[2], q[3], q[0]))
    slot = {q: s for s, q in enumerate(pieces)}
    children = [[] for _ in pieces]
    for q in pieces:
        came = way(q)
        if came is not None:
            parent, axis, side = came
            children[slot[parent]].append((slot[q], axis, -side))
    return children


CHILDREN = piece_table()
PIECES = len(CHILDREN)
STEPS = PIECES // GROUP


def unit_scale(wide):
    return lax.rsqrt(jnp.sum(wide * wide, axis=-1, keepdims=True) + epsilon)


def unit_kernel(caps_ref, tests_ref, caps_out, tests_out):
    wide = caps_ref[...].astype(jnp.float32)
    caps_out[...] = (wide * (unit_scale(wide) * exp2_scale)).astype(jnp.bfloat16)
    wide = tests_ref[...].astype(jnp.float32)
    tests_out[...] = (wide * unit_scale(wide)).astype(jnp.bfloat16)


def gather_kernel(
    caps_ref, tests_ref, gallery_ref, all_tests_ref, columns_ref, log_ref,
    caps, tests, clips, acc, share, others,
    send_sem, recv_sem, tsend_sem, trecv_sem, bsend_sem, brecv_sem, local_sem,
):
    bank = lax.axis_index("bank")
    gal = lax.axis_index("gal")
    y_hi, core = bank // 2, bank % 2
    z, y_lo, x = gal // 8, (gal // 4) % 2, gal % 4
    y = y_hi * 2 + y_lo

    def at(axis, step):
        if axis == "x":
            return {"bank": bank, "gal": z * 8 + y_lo * 4 + (x + step + 4) % 4}
        if axis == "z":
            return {"bank": bank, "gal": ((z + step + 4) % 4) * 8 + y_lo * 4 + x}
        new_y = (y + step + 4) % 4
        return {"bank": (new_y // 2) * 2 + core, "gal": z * 8 + (new_y % 2) * 4 + x}

    partner = {"bank": bank, "gal": z * 8 + (1 - y_lo) * 4 + x}
    sibling = {"bank": y_hi * 2 + 1 - core, "gal": gal}

    load = pltpu.make_async_copy(gallery_ref, clips, local_sem.at[0])
    load.start()

    barrier = pltpu.get_barrier_semaphore()
    peers = [at("x", 1), at("x", -1), at("z", 1), at("z", -1), at("y", 1), at("y", -1)]
    peers += [{"bank": (bank + k) % 4, "gal": gal} for k in (1, 2, 3)]
    for peer in peers:
        pl.semaphore_signal(barrier, inc=1, device_id=peer, device_id_type=MESH)
    pl.semaphore_wait(barrier, len(peers))

    def send_of(source, target, axis, step):
        device = partner if axis == "y" else at(axis, step)
        return pltpu.make_async_remote_copy(
            src_ref=source,
            dst_ref=caps.at[target],
            send_sem=send_sem.at[target],
            recv_sem=recv_sem.at[target],
            device_id=device,
            device_id_type=MESH,
        )

    def own(piece):
        return caps_ref.at[pl.ds(piece * PIECE, PIECE), :]

    def forward(piece):
        source = own(piece) if piece < 2 else caps.at[piece]
        for target, axis, step in CHILDREN[piece]:
            send_of(source, target, axis, step).start()

    def arrive(piece):
        send_of(caps.at[piece], piece, "x", 1).wait_recv()
        forward(piece)

    def test_copy(index, part, device):
        return pltpu.make_async_remote_copy(
            src_ref=part, dst_ref=part,
            send_sem=tsend_sem.at[index], recv_sem=trecv_sem.at[index],
            device_id=device, device_id_type=MESH,
        )

    def minus(value, step):
        return (value - step + 4) % 4

    def y_block(value):
        return tests.at[(value // 2) * 2 + core, :, value % 2]

    def y_half(value, half):
        return tests.at[(value // 2) * 2 + core, pl.ds(half * 2, 2), value % 2]

    def test_sends(stage):
        mine = tests.at[bank, z, y_lo, x]
        if stage == 0:
            return [(0, tests_ref, mine, at("x", 1)), (1, tests_ref, mine, at("x", -1))]
        if stage == 1:
            part = tests.at[bank, z, y_lo, minus(x, 1)]
            return [(2, part, part, at("x", 1))]
        if stage == 2:
            part = tests.at[bank, z, y_lo]
            return [(3, part, part, at("z", 1)), (4, part, part, at("z", -1))]
        if stage == 3:
            up = tests.at[bank, minus(z, 1), y_lo, pl.ds(0, 2)]
            down = tests.at[bank, minus(z, -1), y_lo, pl.ds(2, 2)]
            return [(5, up, up, at("z", 1)), (6, down, down, at("z", -1))]
        if stage == 4:
            part = y_block(y)
            return [(7, part, part, at("y", 1)), (8, part, part, at("y", -1))]
        if stage == 5:
            up, down = y_half(minus(y, 1), 0), y_half(minus(y, -1), 1)
            return [(9, up, up, at("y", 1)), (10, down, down, at("y", -1))]
        low, high = tests.at[core], tests.at[2 + core]
        return [(11, low, low, sibling), (12, high, high, sibling)]

    def test_start(stage):
        for index, source, target, device in test_sends(stage):
            pltpu.make_async_remote_copy(
                src_ref=source, dst_ref=target,
                send_sem=tsend_sem.at[index], recv_sem=trecv_sem.at[index],
                device_id=device, device_id_type=MESH,
            ).start()

    def test_arrive(stage):
        for index, source, target, device in test_sends(stage):
            if stage == 0:
                part = tests.at[bank, z, y_lo, minus(x, 1 if index == 0 else -1)]
            elif stage == 1:
                part = tests.at[bank, z, y_lo, minus(x, 2)]
            elif stage == 2:
                part = tests.at[bank, minus(z, 1 if index == 3 else -1), y_lo]
            elif stage == 3:
                part = tests.at[bank, minus(z, 2), y_lo, pl.ds(0 if index == 5 else 2, 2)]
            elif stage == 4:
                part = y_block(minus(y, 1 if index == 7 else -1))
            elif stage == 5:
                part = y_half(minus(y, 2), 0 if index == 9 else 1)
            else:
                part = tests.at[(0 if index == 11 else 2) + 1 - core]
            test_copy(index, part, sibling).wait_recv()

    forward(0)
    forward(1)
    test_start(0)
    caps[0] = caps_ref[0:PIECE, :]
    caps[1] = caps_ref[PIECE : 2 * PIECE, :]
    tests[bank, z, y_lo, x] = tests_ref[...]
    acc[...] = jnp.zeros_like(acc)

    load.wait()

    def unit_block(index, carry):
        rows = pl.ds(pl.multiple_of(index * 256, 256), 256)
        wide = clips[rows, :].astype(jnp.float32)
        clips[rows, :] = (wide * unit_scale(wide)).astype(jnp.bfloat16)
        return carry

    lax.fori_loop(0, clips.shape[0] // 256, unit_block, 0)

    share_rows = columns_ref.shape[0]
    columns_copy = pltpu.make_async_copy(
        clips.at[pl.ds(pl.multiple_of(bank * share_rows, share_rows), share_rows), :],
        columns_ref,
        local_sem.at[1],
    )

    test_steps = {2: 0, 3: 1, 5: 2, 7: 3, 11: 4, 14: 5}

    def move(step):
        for piece in range(GROUP * step, GROUP * (step + 1)):
            if piece >= 2:
                arrive(piece)
        if step == 1:
            columns_copy.start()
        if step in test_steps:
            test_arrive(test_steps[step])
            test_start(test_steps[step] + 1)

    def choose(step, low, high):
        if high - low == 1:
            move(low)
            return
        middle = (low + high) // 2

        @pl.when(step < middle)
        def _():
            choose(step, low, middle)

        @pl.when(step >= middle)
        def _():
            choose(step, middle, high)

    def one_step(step, carry):
        choose(step, 0, STEPS)
        block = caps[pl.ds(step * GROUP, GROUP)].reshape(GROUP * PIECE, D)
        sims = lax.dot_general(
            block, clips[...], (((1,), (1,)), ((), ())), preferred_element_type=jnp.float32
        )
        terms = jnp.exp2(sims).reshape(GROUP * PIECE // 8, 8, sims.shape[1])
        acc[...] += jnp.sum(terms, axis=0)
        return carry

    lax.fori_loop(0, STEPS, one_step, 0)

    sums = jnp.sum(acc[...], axis=0, keepdims=True)
    for k in range(4):
        share[k] = sums[:, k * share_rows : (k + 1) * share_rows]

    def bank_copy(k):
        peer = (bank + k) % 4
        return pltpu.make_async_remote_copy(
            src_ref=share.at[peer], dst_ref=others.at[k - 1],
            send_sem=bsend_sem.at[k - 1], recv_sem=brecv_sem.at[k - 1],
            device_id={"bank": peer, "gal": gal}, device_id_type=MESH,
        )

    for k in (2, 1, 3):
        bank_copy(k).start()

    test_arrive(6)
    tests_copy = pltpu.make_async_copy(tests, all_tests_ref, local_sem.at[2])
    tests_copy.start()

    for k in (1, 3, 2):
        bank_copy(k).wait_recv()
    total = share[bank] + others[0] + others[1] + others[2]
    count = 4 * 32 * caps_ref.shape[0]
    log_ref[...] = jnp.log(total / count)

    for k in (1, 2, 3):
        bank_copy(k).wait_send()
    for piece in range(PIECES):
        source = own(piece) if piece < 2 else caps.at[piece]
        for target, axis, step in CHILDREN[piece]:
            send_of(source, target, axis, step).wait_send()
    for stage in range(7):
        for index, source, target, device in test_sends(stage):
            test_copy(index, target, device).wait_send()
    columns_copy.wait()
    tests_copy.wait()


def score_kernel(tests_ref, columns_ref, log_ref, out_ref):
    sims = lax.dot_general(
        tests_ref[...], columns_ref[...], (((1,), (1,)), ((), ())), preferred_element_type=jnp.float32
    )
    result = inverse_temp * sims - log_ref[...]
    out_ref[...] = result.reshape(out_ref.shape)


def local(querybank, gallery, test_queries):
    vmem = pl.BlockSpec(memory_space=pltpu.VMEM)
    anywhere = pl.BlockSpec(memory_space=pl.ANY)
    bf16, f32 = jnp.bfloat16, jnp.float32
    clip_rows = gallery.shape[0]
    share_rows = clip_rows // 4
    test_rows = test_queries.shape[0] * 128
    caps, tests = pl.pallas_call(
        unit_kernel,
        out_shape=(
            jax.ShapeDtypeStruct(querybank.shape, bf16),
            jax.ShapeDtypeStruct(test_queries.shape, bf16),
        ),
        in_specs=[vmem, vmem],
        out_specs=(vmem, vmem),
    )(querybank, test_queries)
    tests_shape = (4, 4, 2, 4, test_queries.shape[0], D)
    every_test, columns, logs = pl.pallas_call(
        gather_kernel,
        out_shape=(
            jax.ShapeDtypeStruct(tests_shape, bf16),
            jax.ShapeDtypeStruct((share_rows, D), bf16),
            jax.ShapeDtypeStruct((1, share_rows), f32),
        ),
        in_specs=[vmem, vmem, anywhere],
        out_specs=(anywhere, anywhere, vmem),
        scratch_shapes=[
            pltpu.VMEM((PIECES, PIECE, D), bf16),
            pltpu.VMEM(tests_shape, bf16),
            pltpu.VMEM((clip_rows, D), bf16),
            pltpu.VMEM((8, clip_rows), f32),
            pltpu.VMEM((4, 1, share_rows), f32),
            pltpu.VMEM((3, 1, share_rows), f32),
            pltpu.SemaphoreType.DMA((PIECES,)),
            pltpu.SemaphoreType.DMA((PIECES,)),
            pltpu.SemaphoreType.DMA((13,)),
            pltpu.SemaphoreType.DMA((13,)),
            pltpu.SemaphoreType.DMA((3,)),
            pltpu.SemaphoreType.DMA((3,)),
            pltpu.SemaphoreType.DMA((3,)),
        ],
        compiler_params=pltpu.CompilerParams(
            collective_id=0, has_side_effects=True, vmem_limit_bytes=40 << 20
        ),
    )(caps, tests, gallery)
    block = 256
    result = pl.pallas_call(
        score_kernel,
        grid=(test_rows // block,),
        out_shape=jax.ShapeDtypeStruct((test_rows, 1, share_rows), f32),
        in_specs=[
            pl.BlockSpec((block, D), lambda i: (i, 0)),
            pl.BlockSpec((share_rows, D), lambda i: (0, 0)),
            pl.BlockSpec((1, share_rows), lambda i: (0, 0)),
        ],
        out_specs=pl.BlockSpec((block, 1, share_rows), lambda i: (i, 0, 0)),
        compiler_params=pltpu.CompilerParams(vmem_limit_bytes=40 << 20),
    )(every_test.reshape(test_rows, D), columns, logs)
    return result


def solution(mesh):
    placed = (P(("bank", "gal"), None), P("gal", None), P(("bank", "gal"), None))
    return jax.shard_map(
        local, mesh=mesh, in_specs=placed, out_specs=P(None, "gal", "bank"), check_vma=False
    )
```

time: 501 us -> 63.3 us (0.13)
  waiting for transfers between devices: 376 us -> 0 us
  Pallas kernels: 0 us -> 59.3 us
  matrix products: 42.4 us -> 0 us
  blocking collectives: 32.3 us -> 0 us
  local copies, waits for them, and re-layouts: 22.7 us -> 3.81 us
  other arithmetic: 13.9 us -> 0 us
  between operations: 13.5 us -> 0.01 us
    all_gather x2 -> x0, waiting for transfers between devices: 376 us -> none  [the longest x1 254 us: local(): every_test = lax.all_gather(tests, ('bank', 'gal'), axis=0, tiled=True)]
    pallas_call x0 -> x3, Pallas kernels: none -> 59.3 us  [the longest x1 50.9 us: local(): pl.pallas_call(gather_kernel, out_shape=(jax.ShapeDtypeStruct(tests_shape...]
    dot_general x9 -> x0, matrix products: 42.4 us -> none  [the longest x8 38.2 us: one_block(): sims = jnp.dot(block, clips_t, preferred_element_type=jnp.float32)]
    psum x1 -> x0, blocking collectives: 32.3 us -> none  [local(): totals = lax.psum(partial_sums, 'bank')]
    broadcast_in_dim x1 -> x0, local copies, waits for them, and re-layouts: 16.1 us -> none  [local(): return result[:, None, :]]
    convert_element_type x3 -> x0, other arithmetic: 5.84 us -> none  [unit_rows(): (wide * lax.rsqrt(jnp.sum(wide * wide, axis=-1, keepdims=True) + epsilon)...]
    reduce_sum x3 -> x0, other arithmetic: 5.06 us -> none  [unit_rows(): jnp.sum(wide * wide, axis=-1, keepdims=True) + epsilon]
  transfers between devices with their start and end apart: 2 -> 0, of which waited for: 2 -> 0; matrix products, arithmetic and copies ran while one was open for 11% -> 0% of each run, Pallas kernels for 0% -> 0%
where the time goes in v1:
time: 63.3 us; the launch traced here: 63.1 us
  Pallas kernels  59.3 us (94%)
  local copies, waits for them, and re-layouts  3.81 us (6%)
    pallas_call x1, Pallas kernels, local(): pl.pallas_call(gather_kernel, out_shape=(jax.ShapeDtypeStruct(tests_shape...  50.9 us
    pallas_call x1, Pallas kernels, local(): pl.pallas_call(score_kernel, grid=(test_rows // block,), out_shape=jax.Sh...  6.75 us
    unnamed x6, local copies, waits for them, and re-layouts  3.81 us
    pallas_call x1, Pallas kernels, local(): pl.pallas_call(unit_kernel, out_shape=(jax.ShapeDtypeStruct(querybank.sha...  1.68 us

profile of v1, /device:TPU:1, one launch (start us, length us, event | category | flops | bytes accessed | tf_op | source)
XLA Modules:
  0.0 63.1 jit_solution(8912618397900627610)
XLA Ops:
  0.0 1.7 %shard_map.37 = (bf16[128,512]{1,0:T(8,128)(2,1)}, bf16[16,512]{1,0:T(8,128)(2,1)}) custom-call(bf16[128,512]{1,0:T(8,128)(2,1)} %caps_ref.1, bf16[16,512]{1,0:T(8,128)(2,1)} %tests_ref.1), custom_call_target="tpu_custom_call" | custom-call | tf_op jit(solution)/shard_map/pallas_call | solution.py:312
  1.7 0.0 copy-start
  1.7 2.2 %copy-done = bf16[4096,512]{1,0:T(8,128)(2,1)S(1)} copy-done((bf16[4096,512]{1,0:T(8,128)(2,1)S(1)}, bf16[4096,512]{1,0:T(8,128)(2,1)}, u32[]{:S(2)}) %copy-start) | copy-done | bytes 4194328
  3.9 0.0 copy-start.1
  3.9 0.9 %copy-done.1 = bf16[128,512]{1,0:T(8,128)(2,1)S(1)} copy-done((bf16[128,512]{1,0:T(8,128)(2,1)S(1)}, bf16[128,512]{1,0:T(8,128)(2,1)}, u32[]{:S(2)}) %copy-start.1) | copy-done | bytes 131096
  4.8 0.0 copy-start.2
  4.8 0.7 %copy-done.2 = bf16[16,512]{1,0:T(8,128)(2,1)S(1)} copy-done((bf16[16,512]{1,0:T(8,128)(2,1)S(1)}, bf16[16,512]{1,0:T(8,128)(2,1)}, u32[]{:S(2)}) %copy-start.2) | copy-done | bytes 16408
  5.5 50.9 %shard_map.38 = (bf16[4,4,2,4,16,512]{5,4,3,2,1,0:T(8,128)(2,1)S(1)}, bf16[1024,512]{1,0:T(8,128)(2,1)S(1)}, f32[1,1024]{1,0:T(1,128)S(1)}) custom-call(bf16[128,512]{1,0:T(8,128)(2,1)S(1)} %copy-done.1, bf16[16,512]{1,0:T(8,128)(2,1)S(1)} %copy-done.2, bf16[4096,512]{1,0:T(8,128)(2,1)S(1)} %copy-done), custom_call_target="tpu_custom_call" | custom-call | tf_op jit(solution)/shard_map/pallas_call | solution.py:322
  56.4 6.8 %shard_map.39 = f32[2048,1,1024]{2,1,0:T(1,128)} custom-call(bf16[2048,512]{1,0:T(8,128)(2,1)S(1)} %bitcast.1, bf16[1024,512]{1,0:T(8,128)(2,1)S(1)} %get-tuple-element.13.columns_ref, f32[1,1024]{1,0:T(1,128)S(1)} %get-tuple-element.14.log_ref), custom_call_target="tpu_custom_call" | custom-call | tf_op jit(solution)/shard_map/pallas_call | solution.py:351
Async XLA Ops:
  1.7 2.2 %copy-start = (bf16[4096,512]{1,0:T(8,128)(2,1)S(1)}, bf16[4096,512]{1,0:T(8,128)(2,1)}, u32[]{:S(2)}) copy-start(bf16[4096,512]{1,0:T(8,128)(2,1)} %gallery_ref.1) | copy-start | bytes 12582916
  3.9 0.9 %copy-start.1 = (bf16[128,512]{1,0:T(8,128)(2,1)S(1)}, bf16[128,512]{1,0:T(8,128)(2,1)}, u32[]{:S(2)}) copy-start(bf16[128,512]{1,0:T(8,128)(2,1)} %get-tuple-element.10.caps_ref) | copy-start | bytes 393220
  4.8 0.7 %copy-start.2 = (bf16[16,512]{1,0:T(8,128)(2,1)S(1)}, bf16[16,512]{1,0:T(8,128)(2,1)}, u32[]{:S(2)}) copy-start(bf16[16,512]{1,0:T(8,128)(2,1)} %get-tuple-element.11.tests_ref) | copy-start | bytes 49156

commit v2 on v1

v2 whole, which is shorter than its diff:
```python
import functools
import math

import jax
import jax.numpy as jnp
from jax import lax
from jax.experimental import pallas as pl
from jax.experimental.pallas import tpu as pltpu
from jax.sharding import PartitionSpec as P

MESH = pl.DeviceIdType.MESH
inverse_temp = 20.0
epsilon = 1e-06
exp2_scale = inverse_temp * math.log2(math.e)

D = 512
PIECE = 64
GROUP = 4
RING = 4


ORDER = (
    0, 1, 6, 32, 3, 24, 2, 9, 7, 25, 34, 33, 40, 8, 26, 30,
    11, 15, 57, 56, 17, 38, 5, 39, 14, 48, 41, 62, 35, 13, 27, 16,
    28, 63, 59, 10, 19, 31, 43, 58, 36, 47, 46, 42, 4, 49, 54, 18,
    21, 44, 29, 50, 45, 61, 55, 37, 52, 23, 60, 51, 12, 53, 22, 20,
)
AHEAD = (
    0, 0, 0, 1, 0, 2, 0, 0, 0, 0, 0, 1, 0, 2, 0, 0,
    0, 0, 0, 2, 0, 0, 0, 1, 1, 0, 0, 0, 1, 0, 0, 0,
    0, 0, 0, 0, 1, 2, 0, 2, 0, 0, 1, 2, 2, 2, 0, 0,
    0, 0, 1, 1, 0, 0, 1, 0, 0, 0, 2, 1, 2, 0, 0, 0,
)


def piece_table():
    pieces = [(code % 2, code // 32, code // 8 % 4, code // 2 % 4) for code in ORDER]

    def way(piece):
        kind, dy, p1, p2 = piece
        if p2:
            side = p2 if p2 != 2 else (1 if (dy + p1) % 2 == 0 else 3)
            parent = (kind, dy, p1, (p2 - side) % RING)
            return parent, ("x", "z")[1 - kind], side
        if p1:
            side = p1 if p1 != 2 else (1 if dy == 0 else 3)
            parent = (kind, dy, (p1 - side) % RING, 0)
            return parent, ("x", "z")[kind], side
        if dy:
            return (kind, 0, 0, 0), "y", 1
        return None

    slot = {q: s for s, q in enumerate(pieces)}
    children = [[] for _ in pieces]
    for q in pieces:
        came = way(q)
        if came is not None:
            parent, axis, side = came
            children[slot[parent]].append((slot[q], axis, -side))
    return children


CHILDREN = piece_table()
PIECES = len(CHILDREN)
STEPS = PIECES // GROUP
HANDLED = [
    [s for s in range(2, PIECES) if max(0, s // GROUP - AHEAD[s]) == step] for step in range(STEPS)
]


def unit_scale(wide):
    return lax.rsqrt(jnp.sum(wide * wide, axis=-1, keepdims=True) + epsilon)


def gather_kernel(
    caps_ref, tests_ref, gallery_ref, all_tests_ref, columns_ref, log_ref,
    raw_caps, raw_tests, caps, tests, clips, acc, share, others,
    send_sem, recv_sem, tsend_sem, trecv_sem, bsend_sem, brecv_sem, local_sem,
):
    bank = lax.axis_index("bank")
    gal = lax.axis_index("gal")
    y_hi, core = bank // 2, bank % 2
    z, y_lo, x = gal // 8, (gal // 4) % 2, gal % 4
    y = y_hi * 2 + y_lo

    def at(axis, step):
        if axis == "x":
            return {"bank": bank, "gal": z * 8 + y_lo * 4 + (x + step + 4) % 4}
        if axis == "z":
            return {"bank": bank, "gal": ((z + step + 4) % 4) * 8 + y_lo * 4 + x}
        new_y = (y + step + 4) % 4
        return {"bank": (new_y // 2) * 2 + core, "gal": z * 8 + (new_y % 2) * 4 + x}

    partner = {"bank": bank, "gal": z * 8 + (1 - y_lo) * 4 + x}
    sibling = {"bank": y_hi * 2 + 1 - core, "gal": gal}

    barrier = pltpu.get_barrier_semaphore()
    peers = [at("x", 1), at("x", -1), at("z", 1), at("z", -1), at("y", 1), at("y", -1)]
    peers += [{"bank": (bank + k) % 4, "gal": gal} for k in (1, 2, 3)]
    for peer in peers:
        pl.semaphore_signal(barrier, inc=1, device_id=peer, device_id_type=MESH)

    load_caps = pltpu.make_async_copy(caps_ref, raw_caps, local_sem.at[3])
    load_tests = pltpu.make_async_copy(tests_ref, raw_tests, local_sem.at[4])
    load = pltpu.make_async_copy(gallery_ref, clips, local_sem.at[0])
    load_caps.start()
    load_tests.start()
    load.start()
    load_caps.wait()
    wide = raw_caps[...].astype(jnp.float32)
    unit = (wide * (unit_scale(wide) * exp2_scale)).astype(jnp.bfloat16)
    caps[0] = unit[0:PIECE, :]
    caps[1] = unit[PIECE : 2 * PIECE, :]
    load_tests.wait()
    wide = raw_tests[...].astype(jnp.float32)
    tests[bank, z, y_lo, x] = (wide * unit_scale(wide)).astype(jnp.bfloat16)
    acc[...] = jnp.zeros_like(acc)
    pl.semaphore_wait(barrier, len(peers))

    def send_of(source, target, axis, step):
        device = partner if axis == "y" else at(axis, step)
        return pltpu.make_async_remote_copy(
            src_ref=source,
            dst_ref=caps.at[target],
            send_sem=send_sem.at[target],
            recv_sem=recv_sem.at[target],
            device_id=device,
            device_id_type=MESH,
        )

    def forward(piece):
        for target, axis, step in CHILDREN[piece]:
            send_of(caps.at[piece], target, axis, step).start()

    def arrive(piece):
        send_of(caps.at[piece], piece, "x", 1).wait_recv()
        forward(piece)

    def block(step_y, step_z, first, last):
        yy, zz = (y + step_y + 4) % 4, (z + step_z + 4) % 4
        part = tests.at[(yy // 2) * 2 + core, zz, yy % 2]
        return part if last - first == 4 else part.at[pl.ds(first, last - first)]

    def test_message(index):
        if index < 3:
            step = (1, -1, 1)[index]
            offset = (0, 0, -1)[index]
            row = tests.at[bank, z, y_lo]
            return row.at[(x + offset + 4) % 4], row.at[(x + offset - step + 4) % 4], at("x", step)
        if index < 7:
            step = (1, -1, 1, -1)[index - 3]
            offset = (0, 0, -1, 1)[index - 3]
            first, last = ((0, 4), (0, 4), (0, 2), (2, 4))[index - 3]
            return block(0, offset, first, last), block(0, offset - step, first, last), at("z", step)
        if index < 23:
            zz = (0, -1, 1, 2)[(index - 7) // 4]
            kind = (index - 7) % 4
            step = (1, -1, 1, -1)[kind]
            offset = (0, 0, -1, 1)[kind]
            first, last = ((0, 4), (0, 4), (0, 2), (2, 4))[kind]
            return block(offset, zz, first, last), block(offset - step, zz, first, last), at("y", step)
        yy = (y + (0, 1, -1, 2)[index - 23] + 4) % 4
        low = (yy // 2) * 2
        return tests.at[low + core, :, yy % 2], tests.at[low + 1 - core, :, yy % 2], sibling

    def test_copy(index, arriving):
        sent, arrives, device = test_message(index)
        part = arrives if arriving else sent
        return pltpu.make_async_remote_copy(
            src_ref=part, dst_ref=part,
            send_sem=tsend_sem.at[index], recv_sem=trecv_sem.at[index],
            device_id=device, device_id_type=MESH,
        )

    def test_start(*indices):
        for index in indices:
            test_copy(index, False).start()

    def test_arrive(*indices):
        for index in indices:
            test_copy(index, True).wait_recv()

    test_start(0, 1)
    forward(0)
    forward(1)

    load.wait()

    def unit_block(index, carry):
        rows = pl.ds(pl.multiple_of(index * 256, 256), 256)
        wide = clips[rows, :].astype(jnp.float32)
        clips[rows, :] = (wide * unit_scale(wide)).astype(jnp.bfloat16)
        return carry

    lax.fori_loop(0, clips.shape[0] // 256, unit_block, 0)

    share_rows = columns_ref.shape[0]
    columns_copy = pltpu.make_async_copy(
        clips.at[pl.ds(pl.multiple_of(bank * share_rows, share_rows), share_rows), :],
        columns_ref,
        local_sem.at[1],
    )

    def move_tests(step):
        if step == 0:
            test_arrive(0, 1)
            test_start(2)
        if step == 2:
            test_arrive(2)
            test_start(3, 4, 7, 8)
        if step == 6:
            test_arrive(3, 4)
            test_start(5, 6, 11, 12, 15, 16)
            test_arrive(7, 8)
            test_start(9, 10)
        if step == 10:
            test_arrive(5, 6)
            test_start(19, 20)
            test_arrive(11, 12, 15, 16)
            test_start(13, 14, 17, 18)
        if step == 13:
            test_arrive(19, 20)
            test_start(21, 22, 23, 24, 25)

    def move(step):
        move_tests(step)
        for piece in HANDLED[step]:
            arrive(piece)
        if step == 1:
            columns_copy.start()

    def choose(step, low, high):
        if high - low == 1:
            move(low)
            return
        middle = (low + high) // 2

        @pl.when(step < middle)
        def _():
            choose(step, low, middle)

        @pl.when(step >= middle)
        def _():
            choose(step, middle, high)

    def one_step(step, carry):
        choose(step, 0, STEPS)
        block = caps[pl.ds(step * GROUP, GROUP)].reshape(GROUP * PIECE, D)
        sims = lax.dot_general(
            block, clips[...], (((1,), (1,)), ((), ())), preferred_element_type=jnp.float32
        )
        terms = jnp.exp2(sims).reshape(GROUP * PIECE // 8, 8, sims.shape[1])
        acc[...] += jnp.sum(terms, axis=0)
        return carry

    lax.fori_loop(0, STEPS, one_step, 0)

    sums = jnp.sum(acc[...], axis=0, keepdims=True)
    for k in range(4):
        share[k] = sums[:, k * share_rows : (k + 1) * share_rows]

    def bank_copy(k):
        peer = (bank + k) % 4
        return pltpu.make_async_remote_copy(
            src_ref=share.at[peer], dst_ref=others.at[k - 1],
            send_sem=bsend_sem.at[k - 1], recv_sem=brecv_sem.at[k - 1],
            device_id={"bank": peer, "gal": gal}, device_id_type=MESH,
        )

    for k in (2, 1, 3):
        bank_copy(k).start()

    test_arrive(9, 10, 13, 14, 17, 18, 21, 22)
    test_start(26)
    test_arrive(23, 24, 25, 26)
    tests_copy = pltpu.make_async_copy(tests, all_tests_ref, local_sem.at[2])
    tests_copy.start()

    for k in (1, 3, 2):
        bank_copy(k).wait_recv()
    total = share[bank] + others[0] + others[1] + others[2]
    count = 4 * 32 * caps_ref.shape[0]
    log_ref[...] = jnp.log(total / count)

    for k in (1, 2, 3):
        bank_copy(k).wait_send()
    for piece in range(PIECES):
        for target, axis, step in CHILDREN[piece]:
            send_of(caps.at[piece], target, axis, step).wait_send()
    for index in range(27):
        test_copy(index, False).wait_send()
    columns_copy.wait()
    tests_copy.wait()


def score_kernel(tests_ref, columns_ref, log_ref, out_ref):
    sims = lax.dot_general(
        tests_ref[...], columns_ref[...], (((1,), (1,)), ((), ())), preferred_element_type=jnp.float32
    )
    result = inverse_temp * sims - log_ref[...]
    out_ref[...] = result.reshape(out_ref.shape)


def local(querybank, gallery, test_queries):
    vmem = pl.BlockSpec(memory_space=pltpu.VMEM)
    anywhere = pl.BlockSpec(memory_space=pl.ANY)
    hbm = pl.BlockSpec(memory_space=pltpu.MemorySpace.HBM)
    bf16, f32 = jnp.bfloat16, jnp.float32
    clip_rows = gallery.shape[0]
    share_rows = clip_rows // 4
    test_rows = test_queries.shape[0] * 128
    tests_shape = (4, 4, 2, 4, test_queries.shape[0], D)
    every_test, columns, logs = pl.pallas_call(
        gather_kernel,
        out_shape=(
            jax.ShapeDtypeStruct(tests_shape, bf16),
            jax.ShapeDtypeStruct((share_rows, D), bf16),
            jax.ShapeDtypeStruct((1, share_rows), f32),
        ),
        in_specs=[hbm, hbm, hbm],
        out_specs=(anywhere, anywhere, vmem),
        scratch_shapes=[
            pltpu.VMEM(querybank.shape, bf16),
            pltpu.VMEM(test_queries.shape, bf16),
            pltpu.VMEM((PIECES, PIECE, D), bf16),
            pltpu.VMEM(tests_shape, bf16),
            pltpu.VMEM((clip_rows, D), bf16),
            pltpu.VMEM((8, clip_rows), f32),
            pltpu.VMEM((4, 1, share_rows), f32),
            pltpu.VMEM((3, 1, share_rows), f32),
            pltpu.SemaphoreType.DMA((PIECES,)),
            pltpu.SemaphoreType.DMA((PIECES,)),
            pltpu.SemaphoreType.DMA((27,)),
            pltpu.SemaphoreType.DMA((27,)),
            pltpu.SemaphoreType.DMA((3,)),
            pltpu.SemaphoreType.DMA((3,)),
            pltpu.SemaphoreType.DMA((5,)),
        ],
        compiler_params=pltpu.CompilerParams(
            collective_id=0, has_side_effects=True, vmem_limit_bytes=40 << 20
        ),
    )(*(pltpu.with_memory_space_constraint(a, pltpu.MemorySpace.HBM) for a in (querybank, test_queries, gallery)))
    block = 256
    result = pl.pallas_call(
        score_kernel,
        grid=(test_rows // block,),
        out_shape=jax.ShapeDtypeStruct((test_rows, 1, share_rows), f32),
        in_specs=[
            pl.BlockSpec((block, D), lambda i: (i, 0)),
            pl.BlockSpec((share_rows, D), lambda i: (0, 0)),
            pl.BlockSpec((1, share_rows), lambda i: (0, 0)),
        ],
        out_specs=pl.BlockSpec((block, 1, share_rows), lambda i: (i, 0, 0)),
        compiler_params=pltpu.CompilerParams(vmem_limit_bytes=40 << 20),
    )(every_test.reshape(test_rows, D), columns, logs)
    return result


def solution(mesh):
    placed = (P(("bank", "gal"), None), P("gal", None), P(("bank", "gal"), None))
    return jax.shard_map(
        local, mesh=mesh, in_specs=placed, out_specs=P(None, "gal", "bank"), check_vma=False
    )
```

time: 63.3 us -> 51 us (0.81)
  Pallas kernels: 59.3 us -> 50.9 us
  local copies, waits for them, and re-layouts: 3.81 us -> 0 us
    pallas_call x1, Pallas kernels: 50.9 us -> 44.2 us  [local(): pl.pallas_call(gather_kernel, out_shape=(jax.ShapeDtypeStruct(tests_shape...]
    unnamed x6 -> x0, local copies, waits for them, and re-layouts: 3.81 us -> none
    pallas_call x1 -> x0, Pallas kernels: 1.68 us -> none  [local(): pl.pallas_call(unit_kernel, out_shape=(jax.ShapeDtypeStruct(querybank.sha...]
where the time goes in v2:
time: 51 us; the launch traced here: 50.9 us
  Pallas kernels  50.9 us (100%)
    pallas_call x1, Pallas kernels, local(): pl.pallas_call(gather_kernel, out_shape=(jax.ShapeDtypeStruct(tests_shape...  44.2 us
    pallas_call x1, Pallas kernels, local(): pl.pallas_call(score_kernel, grid=(test_rows // block,), out_shape=jax.Sh...  6.75 us

profile of v2, /device:TPU:1, one launch (start us, length us, event | category | flops | bytes accessed | tf_op | source)
XLA Modules:
  0.0 50.9 jit_solution(18317342442588041951)
XLA Ops:
  0.0 44.2 %shard_map.37 = (bf16[4,4,2,4,16,512]{5,4,3,2,1,0:T(8,128)(2,1)S(1)}, bf16[1024,512]{1,0:T(8,128)(2,1)S(1)}, f32[1,1024]{1,0:T(1,128)S(1)}) custom-call(bf16[128,512]{1,0:T(8,128)(2,1)} %caps_ref.1, bf16[16,512]{1,0:T(8,128)(2,1)} %tests_ref.1, bf16[4096,512]{1,0:T(8,128)(2,1)} %gallery_ref.1), custom_call_target="tpu_custom_call" | custom-call | tf_op jit(solution)/shard_map/pallas_call | solution.py:313
  44.2 6.7 %shard_map.38 = f32[2048,1,1024]{2,1,0:T(1,128)} custom-call(bf16[2048,512]{1,0:T(8,128)(2,1)S(1)} %bitcast.1, bf16[1024,512]{1,0:T(8,128)(2,1)S(1)} %get-tuple-element.9.columns_ref, f32[1,1024]{1,0:T(1,128)S(1)} %get-tuple-element.10.log_ref), custom_call_target="tpu_custom_call" | custom-call | tf_op jit(solution)/shard_map/pallas_call | solution.py:344

commit v3 on v2

--- a/solution.py
+++ b/solution.py
@@ -15,21 +15,21 @@
 
 D = 512
 PIECE = 64
-GROUP = 4
+SIZES = (2,) + 7 * (4,) + 4 * (8,) + (2,)
 RING = 4
 
 
 ORDER = (
-    0, 1, 6, 32, 3, 24, 2, 9, 7, 25, 34, 33, 40, 8, 26, 30,
-    11, 15, 57, 56, 17, 38, 5, 39, 14, 48, 41, 62, 35, 13, 27, 16,
-    28, 63, 59, 10, 19, 31, 43, 58, 36, 47, 46, 42, 4, 49, 54, 18,
-    21, 44, 29, 50, 45, 61, 55, 37, 52, 23, 60, 51, 12, 53, 22, 20,
+    0, 1, 32, 33, 25, 6, 24, 2, 34, 8, 9, 4, 3, 57, 31, 56,
+    39, 40, 27, 35, 14, 41, 15, 10, 63, 17, 26, 11, 49, 7, 46, 48,
+    59, 42, 38, 16, 30, 43, 58, 12, 47, 5, 51, 19, 18, 13, 22, 50,
+    23, 55, 54, 45, 62, 61, 60, 20, 44, 28, 29, 37, 36, 21, 52, 53,
 )
 AHEAD = (
-    0, 0, 0, 1, 0, 2, 0, 0, 0, 0, 0, 1, 0, 2, 0, 0,
-    0, 0, 0, 2, 0, 0, 0, 1, 1, 0, 0, 0, 1, 0, 0, 0,
-    0, 0, 0, 0, 1, 2, 0, 2, 0, 0, 1, 2, 2, 2, 0, 0,
-    0, 0, 1, 1, 0, 0, 1, 0, 0, 0, 2, 1, 2, 0, 0, 0,
+    0, 0, 1, 0, 0, 0, 0, 2, 0, 1, 2, 0, 2, 0, 0, 0,
+    0, 1, 0, 0, 0, 1, 0, 0, 0, 0, 0, 0, 0, 0, 0, 0,
+    1, 0, 0, 1, 0, 0, 0, 0, 0, 0, 0, 0, 0, 0, 0, 0,
+    0, 0, 0, 0, 1, 0, 0, 0, 1, 0, 1, 0, 0, 0, 0, 0,
 )
 
 
@@ -62,9 +62,11 @@
 
 CHILDREN = piece_table()
 PIECES = len(CHILDREN)
-STEPS = PIECES // GROUP
+STEPS = len(SIZES)
+FIRSTS = [sum(SIZES[:step]) for step in range(STEPS)]
+STEP_OF = [step for step in range(STEPS) for unused in range(SIZES[step])]
 HANDLED = [
-    [s for s in range(2, PIECES) if max(0, s // GROUP - AHEAD[s]) == step] for step in range(STEPS)
+    [s for s in range(2, PIECES) if max(0, STEP_OF[s] - AHEAD[s]) == step] for step in range(STEPS)
 ]
 
 
@@ -73,7 +75,7 @@
 
 
 def gather_kernel(
-    caps_ref, tests_ref, gallery_ref, all_tests_ref, columns_ref, log_ref,
+    caps_ref, tests_ref, gallery_ref, scores_ref, log_ref,
     raw_caps, raw_tests, caps, tests, clips, acc, share, others,
     send_sem, recv_sem, tsend_sem, trecv_sem, bsend_sem, brecv_sem, local_sem,
 ):
@@ -194,12 +196,7 @@
 
     lax.fori_loop(0, clips.shape[0] // 256, unit_block, 0)
 
-    share_rows = columns_ref.shape[0]
-    columns_copy = pltpu.make_async_copy(
-        clips.at[pl.ds(pl.multiple_of(bank * share_rows, share_rows), share_rows), :],
-        columns_ref,
-        local_sem.at[1],
-    )
+    share_rows = log_ref.shape[1]
 
     def move_tests(step):
         if step == 0:
@@ -208,17 +205,17 @@
         if step == 2:
             test_arrive(2)
             test_start(3, 4, 7, 8)
-        if step == 6:
+        if step == 7:
             test_arrive(3, 4)
             test_start(5, 6, 11, 12, 15, 16)
             test_arrive(7, 8)
             test_start(9, 10)
-        if step == 10:
+        if step == 9:
             test_arrive(5, 6)
             test_start(19, 20)
             test_arrive(11, 12, 15, 16)
             test_start(13, 14, 17, 18)
-        if step == 13:
+        if step == 11:
             test_arrive(19, 20)
             test_start(21, 22, 23, 24, 25)
 
@@ -226,8 +223,6 @@
         move_tests(step)
         for piece in HANDLED[step]:
             arrive(piece)
-        if step == 1:
-            columns_copy.start()
 
     def choose(step, low, high):
         if high - low == 1:
@@ -243,17 +238,31 @@
         def _():
             choose(step, middle, high)
 
-    def one_step(step, carry):
-        choose(step, 0, STEPS)
-        block = caps[pl.ds(step * GROUP, GROUP)].reshape(GROUP * PIECE, D)
+    def multiply(first, count):
+        rows = caps[pl.ds(first, count)].reshape(count * PIECE, D)
         sims = lax.dot_general(
-            block, clips[...], (((1,), (1,)), ((), ())), preferred_element_type=jnp.float32
-        )
-        terms = jnp.exp2(sims).reshape(GROUP * PIECE // 8, 8, sims.shape[1])
+            rows, clips[...], (((1,), (1,)), ((), ())), preferred_element_type=jnp.float32
+        )
+        terms = jnp.exp2(sims).reshape(count * PIECE // 8, 8, sims.shape[1])
         acc[...] += jnp.sum(terms, axis=0)
-        return carry
-
-    lax.fori_loop(0, STEPS, one_step, 0)
+
+    def run_steps(low, high):
+        if high - low == 1:
+            move(low)
+            multiply(FIRSTS[low], SIZES[low])
+            return
+
+        def one_step(step, carry):
+            choose(step, low, high)
+            multiply(FIRSTS[low] + (step - low) * SIZES[low], SIZES[low])
+            return carry
+
+        lax.fori_loop(low, high, one_step, 0)
+
+    run_steps(0, 1)
+    run_steps(1, 8)
+    run_steps(8, 12)
+    run_steps(12, 13)
 
     sums = jnp.sum(acc[...], axis=0, keepdims=True)
     for k in range(4):
@@ -272,9 +281,24 @@
 
     test_arrive(9, 10, 13, 14, 17, 18, 21, 22)
     test_start(26)
-    test_arrive(23, 24, 25, 26)
-    tests_copy = pltpu.make_async_copy(tests, all_tests_ref, local_sem.at[2])
-    tests_copy.start()
+    mine = pl.ds(pl.multiple_of(bank * share_rows, share_rows), share_rows)
+
+    def score_block(step, carry):
+        index = 2 * (step % 2) + (core + step // 2) % 2
+
+        @pl.when(step == 2)
+        def _():
+            test_arrive(23, 24, 25, 26)
+
+        rows = tests[index].reshape(scores_ref.shape[0] // 4, D)
+        sims = lax.dot_general(
+            rows, clips[mine, :], (((1,), (1,)), ((), ())), preferred_element_type=jnp.float32
+        )
+        block_rows = pl.ds(index * rows.shape[0], rows.shape[0])
+        scores_ref[block_rows] = (inverse_temp * sims).reshape(rows.shape[0], 1, share_rows)
+        return carry
+
+    lax.fori_loop(0, 4, score_block, 0)
 
     for k in (1, 3, 2):
         bank_copy(k).wait_recv()
@@ -289,36 +313,30 @@
             send_of(caps.at[piece], target, axis, step).wait_send()
     for index in range(27):
         test_copy(index, False).wait_send()
-    columns_copy.wait()
-    tests_copy.wait()
-
-
-def score_kernel(tests_ref, columns_ref, log_ref, out_ref):
-    sims = lax.dot_general(
-        tests_ref[...], columns_ref[...], (((1,), (1,)), ((), ())), preferred_element_type=jnp.float32
-    )
-    result = inverse_temp * sims - log_ref[...]
-    out_ref[...] = result.reshape(out_ref.shape)
+
+
+def score_kernel(scores_ref, log_ref, out_ref):
+    rows = out_ref.shape[0]
+    block = scores_ref[pl.ds(pl.multiple_of(pl.program_id(0) * rows, rows), rows)]
+    out_ref[...] = block - log_ref[...].reshape(1, 1, log_ref.shape[1])
 
 
 def local(querybank, gallery, test_queries):
     vmem = pl.BlockSpec(memory_space=pltpu.VMEM)
-    anywhere = pl.BlockSpec(memory_space=pl.ANY)
     hbm = pl.BlockSpec(memory_space=pltpu.MemorySpace.HBM)
     bf16, f32 = jnp.bfloat16, jnp.float32
     clip_rows = gallery.shape[0]
     share_rows = clip_rows // 4
     test_rows = test_queries.shape[0] * 128
     tests_shape = (4, 4, 2, 4, test_queries.shape[0], D)
-    every_test, columns, logs = pl.pallas_call(
+    scores, logs = pl.pallas_call(
         gather_kernel,
         out_shape=(
-            jax.ShapeDtypeStruct(tests_shape, bf16),
-            jax.ShapeDtypeStruct((share_rows, D), bf16),
+            jax.ShapeDtypeStruct((test_rows, 1, share_rows), f32),
             jax.ShapeDtypeStruct((1, share_rows), f32),
         ),
         in_specs=[hbm, hbm, hbm],
-        out_specs=(anywhere, anywhere, vmem),
+        out_specs=(vmem, vmem),
         scratch_shapes=[
             pltpu.VMEM(querybank.shape, bf16),
             pltpu.VMEM(test_queries.shape, bf16),
@@ -340,19 +358,18 @@
             collective_id=0, has_side_effects=True, vmem_limit_bytes=40 << 20
         ),
     )(*(pltpu.with_memory_space_constraint(a, pltpu.MemorySpace.HBM) for a in (querybank, test_queries, gallery)))
-    block = 256
+    block = 512
     result = pl.pallas_call(
         score_kernel,
         grid=(test_rows // block,),
         out_shape=jax.ShapeDtypeStruct((test_rows, 1, share_rows), f32),
         in_specs=[
-            pl.BlockSpec((block, D), lambda i: (i, 0)),
-            pl.BlockSpec((share_rows, D), lambda i: (0, 0)),
-            pl.BlockSpec((1, share_rows), lambda i: (0, 0)),
+            vmem,
+            vmem,
         ],
         out_specs=pl.BlockSpec((block, 1, share_rows), lambda i: (i, 0, 0)),
         compiler_params=pltpu.CompilerParams(vmem_limit_bytes=40 << 20),
-    )(every_test.reshape(test_rows, D), columns, logs)
+    )(scores, logs)
     return result
 
 

time: 51 us -> 46.7 us (0.916)
  Pallas kernels: 50.9 us -> 46.6 us
    pallas_call x1, Pallas kernels: 6.75 us -> 3.63 us  [local(): pl.pallas_call(score_kernel, grid=(test_rows // block,), out_shape=jax.Sh...]
    pallas_call x1, Pallas kernels: 44.2 us -> 42.9 us  [local(): pl.pallas_call(gather_kernel, out_shape=(jax.ShapeDtypeStruct((test_rows,...]
where the time goes in v3:
time: 46.7 us; the launch traced here: 46.6 us
  Pallas kernels  46.6 us (100%)
    pallas_call x1, Pallas kernels, local(): pl.pallas_call(gather_kernel, out_shape=(jax.ShapeDtypeStruct((test_rows,...  42.9 us
    pallas_call x1, Pallas kernels, local(): pl.pallas_call(score_kernel, grid=(test_rows // block,), out_shape=jax.Sh...  3.63 us

profile of v3, /device:TPU:1, one launch (start us, length us, event | category | flops | bytes accessed | tf_op | source)
XLA Modules:
  0.0 46.6 jit_solution(6212128347701498559)
XLA Ops:
  0.0 42.9 %shard_map.37 = (f32[2048,1,1024]{2,1,0:T(1,128)S(1)}, f32[1,1024]{1,0:T(1,128)S(1)}) custom-call(bf16[128,512]{1,0:T(8,128)(2,1)} %caps_ref.1, bf16[16,512]{1,0:T(8,128)(2,1)} %tests_ref.1, bf16[4096,512]{1,0:T(8,128)(2,1)} %gallery_ref.1), custom_call_target="tpu_custom_call" | custom-call | tf_op jit(solution)/shard_map/pallas_call | solution.py:332
  43.0 3.6 %shard_map.38 = f32[2048,1,1024]{2,1,0:T(1,128)} custom-call(f32[2048,1,1024]{2,1,0:T(1,128)S(1)} %get-tuple-element.7.scores_ref, f32[1,1024]{1,0:T(1,128)S(1)} %get-tuple-element.8.log_ref), custom_call_target="tpu_custom_call" | custom-call | tf_op jit(solution)/shard_map/pallas_call | solution.py:362
